TPU v7x, 256 devices: a whole 4x4x8 slice. The times are simulated.
256 devices in a mesh: lat: 64 (over y, z, x_lo), depth: 4 (over x_hi, core).
Axes of the slice: x: 4 (x_hi: 2, x_lo: 2; x = x_hi * 2 + x_lo), y: 4, z: 8, core: 2. Of those that a mesh axis runs over, the one named last changes fastest.
Arguments:
- thermal_anomaly: float32 [128, 256, 2048], P('depth', 'lat'), may hold values from -6 to 6
- water_anomaly: float32 [128, 256, 2048], P('depth', 'lat'), may hold values from -6 to 6
- substrate_class_label: int32 [256, 2048], P('lat'), may hold values from 0 to 11
- sideways_thermal_spread: float32 [12], replicated, may hold values from 0.1 to 0.6
- sideways_water_factors: float32 [12], replicated, may hold values from 0.1 to 0.9
- thermal_solve_matrix: float32 [128, 128], replicated, may hold values from -0.3 to 1.3, as said below
- water_solve_matrix: float32 [128, 128], replicated, may hold values from -0.3 to 1.3, as said below
Outputs:
- temperature_next: float32 [128, 256, 2048], P('depth', 'lat')
- moisture_next: float32 [128, 256, 2048], P('depth', 'lat')
Inputs may be any that keep to these rules, and one draw needn't show every extreme that they name: `thermal_solve_matrix`: a dense matrix with unit diagonal. `water_solve_matrix`: a dense matrix with unit diagonal.
All inputs are finite; a program needn't handle non-finite values.
Results may differ from a plain program's by a relative error of at most 0.00007.
Values sent between devices are 32-bit elements; how exact they have to be, the bound alone decides.
A program may use at most 128 MiB of HBM per device.

v0:
```python
import jax
import jax.numpy as jnp
from jax import lax
from jax.sharding import PartitionSpec as P

VERTICAL_POINTS = 128
LSUB = 4


RATE = 0.25


def extended(cells, sides, width):
    for axis, dim in sides:
        count = lax.axis_size(axis)
        ends = count - 1
        head = lax.slice_in_dim(cells, 0, width, axis=dim)
        tail = lax.slice_in_dim(cells, cells.shape[dim] - width, cells.shape[dim], axis=dim)
        cells = jnp.concatenate(
            [
                lax.ppermute(tail, axis, [(i, (i + 1) % count) for i in range(ends)]),
                cells,
                lax.ppermute(head, axis, [((i + 1) % count, i) for i in range(ends)]),
            ],
            axis=dim,
        )
    return cells


def cheb_matrix(count):
    index = jnp.arange(count).astype(jnp.float32)
    nodes = jnp.cos(jnp.pi * index / (count - 1))
    ends = jnp.where((index == 0) | (index == count - 1), 2.0, 1.0)
    signs = jnp.where(jnp.arange(count) % 2 == 0, 1.0, -1.0)
    weight = (ends * signs).astype(jnp.float32)
    diagonal = jnp.arange(count)[:, None] == jnp.arange(count)[None, :]
    spread = nodes[:, None] - nodes[None, :]
    off = weight[:, None] / weight[None, :] / jnp.where(diagonal, 1.0, spread)
    off = jnp.where(diagonal, 0.0, off)
    return (off - jnp.diag(jnp.sum(off, axis=1)), nodes)


def lateral_sum(after, before, centre):
    zeros = jnp.zeros_like(centre[..., :1])
    east = jnp.concatenate([centre[..., 1:], zeros], axis=-1)
    west = jnp.concatenate([zeros, centre[..., :-1]], axis=-1)
    return after + before + east + west - 4.0 * centre


def advance(profile_snapshot, lap, kappa_heat, kappa_moist):
    wet = profile_snapshot[1]
    kappa_t = kappa_heat * (1.0 + 0.5 * wet * wet / (1.0 + wet * wet))
    return jnp.stack(
        [
            profile_snapshot[0] + RATE * kappa_t * lap[0],
            profile_snapshot[1] + RATE * kappa_moist * lap[1],
        ]
    )


def column_step(pair, kappa_cols, deriv, nodes, thermal_solve_matrix, water_solve_matrix):
    high = lax.Precision.HIGHEST
    scale = (1.0 - nodes * nodes) / deriv.shape[0]
    flux = kappa_cols[None, :, :] * pair[1]
    drain = jnp.einsum("zk,kmc->zmc", deriv, flux, precision=high)
    drain = drain * scale[:, None, None]
    rhs_heat = pair[0] - 0.25 * drain
    rhs_wet = pair[1] + 0.5 * drain
    new_heat = jnp.einsum("zk,kmc->zmc", thermal_solve_matrix, rhs_heat, precision=high)
    new_wet = jnp.einsum("zk,kmc->zmc", water_solve_matrix, rhs_wet, precision=high)
    return jnp.stack([new_heat, new_wet])


def per_device(
    thermal_anomaly,
    water_anomaly,
    substrate_class_label,
    sideways_thermal_spread,
    sideways_water_factors,
    thermal_solve_matrix,
    water_solve_matrix,
):
    labels = jnp.arange(sideways_thermal_spread.shape[0], dtype=jnp.int32)
    onehot = (substrate_class_label[None, :, :] == labels[:, None, None]).astype(jnp.float32)
    kappa_heat = jnp.sum(onehot * sideways_thermal_spread[:, None, None], axis=0)
    kappa_moist = jnp.sum(onehot * sideways_water_factors[:, None, None], axis=0)
    profile_snapshot = jnp.stack([thermal_anomaly, water_anomaly])
    for step in range(LSUB):
        padded = extended(profile_snapshot, (("lat", 2),), 1)
        lap = lateral_sum(padded[:, :, 2:], padded[:, :, :-2], profile_snapshot)
        profile_snapshot = advance(profile_snapshot, lap, kappa_heat, kappa_moist)
    deriv, nodes = cheb_matrix(VERTICAL_POINTS)
    columns = lax.all_to_all(profile_snapshot, "depth", split_axis=3, concat_axis=1, tiled=True)
    width = columns.shape[3]
    start = lax.axis_index("depth") * width
    kappa_cols = lax.dynamic_slice_in_dim(kappa_moist, start, width, 1)
    solved = column_step(
        columns, kappa_cols, deriv, nodes, thermal_solve_matrix, water_solve_matrix
    )
    result = lax.all_to_all(solved, "depth", split_axis=1, concat_axis=3, tiled=True)
    return (result[0], result[1])


def solution(mesh):
    return jax.shard_map(
        per_device,
        mesh=mesh,
        in_specs=(
            P("depth", "lat", None),
            P("depth", "lat", None),
            P("lat", None),
            P(),
            P(),
            P(),
            P(),
        ),
        out_specs=(P("depth", "lat", None), P("depth", "lat", None)),
        check_vma=False,
    )
```

profile of v0, /device:TPU:98, one launch (start us, length us, event | category | flops | bytes accessed | tf_op | source)
XLA Modules:
  0.0 240.9 jit_solution(8652530585767574618)
XLA Ops:
  0.6 2.8 %copy_bitcast_fusion = (f32[1,32,4,2048]{3,1,2,0:T(8,128)S(1)}, f32[1,32,4,2048]{3,1,2,0:T(8,128)S(1)}) fusion(f32[32,4,2048]{2,1,0:T(4,128)} %param.7, f32[32,4,2048]{2,1,0:T(4,128)} %param.8), kind=kLoop, calls=%fused_computation.136 | loop fusion | bytes 4194304 | tf_op jit(solution)/shard_map/stack | solution.py:87
  3.5 2.4 %collective-permute-start = (f32[2,32,1,2048]{3,1,2,0:T(8,128)S(1)}, f32[2,32,1,2048]{3,1,2,0:T(8,128)S(1)}, u32[]{:S(2)}, u32[]{:S(2)}) collective-permute-start(f32[2,32,1,2048]{3,1,2,0:T(8,128)S(1)} %get-tuple-element.38), channel_id=1, source_target_pairs={{4,0},{8,4},{12,8},{16,12},{20,16},{24,20},{28,24},{32,28},{36,32}... | collective-permute-start | bytes 1572872 | tf_op jit(solution)/shard_map/ppermute | solution.py:23
  6.0 5.6 %collective-permute-start.1 = (f32[2,32,1,2048]{3,1,2,0:T(8,128)S(1)}, f32[2,32,1,2048]{3,1,2,0:T(8,128)S(1)}, u32[]{:S(2)}, u32[]{:S(2)}) collective-permute-start(f32[2,32,1,2048]{3,1,2,0:T(8,128)S(1)} %get-tuple-element.39), channel_id=1, source_target_pairs={{0,4},{4,8},{8,12},{12,16},{16,20},{20,24},{24,28},{28,32},{32,36}... | collective-permute-start | bytes 1572872 | tf_op jit(solution)/shard_map/ppermute | solution.py:21
  12.8 15.6 %collective-permute-done = f32[2,32,1,2048]{3,1,2,0:T(8,128)S(1)} collective-permute-done((f32[2,32,1,2048]{3,1,2,0:T(8,128)S(1)}, f32[2,32,1,2048]{3,1,2,0:T(8,128)S(1)}, u32[]{:S(2)}, u32[]{:S(2)}) %collective-permute-start) | collective-permute-done | bytes 524320 | tf_op jit(solution)/shard_map/ppermute | solution.py:23
  28.4 4.1 %collective-permute-done.1 = f32[2,32,1,2048]{3,1,2,0:T(8,128)S(1)} collective-permute-done((f32[2,32,1,2048]{3,1,2,0:T(8,128)S(1)}, f32[2,32,1,2048]{3,1,2,0:T(8,128)S(1)}, u32[]{:S(2)}, u32[]{:S(2)}) %collective-permute-start.1) | collective-permute-done | bytes 524320 | tf_op jit(solution)/shard_map/ppermute | solution.py:21
  35.5 1.9 collective-permute-start.2
  37.4 6.0 %collective-permute-start.3 = (f32[2,32,1,2048]{3,1,2,0:T(8,128)S(1)}, f32[2,32,1,2048]{3,1,2,0:T(8,128)S(1)}, u32[]{:S(2)}, u32[]{:S(2)}) collective-permute-start(f32[2,32,1,2048]{3,1,2,0:T(8,128)S(1)} %get-tuple-element.35), channel_id=1, source_target_pairs={{0,4},{4,8},{8,12},{12,16},{16,20},{20,24},{24,28},{28,32},{32,36}... | collective-permute-start | bytes 1572872 | tf_op jit(solution)/shard_map/ppermute | solution.py:21
  44.2 16.1 %collective-permute-done.2 = f32[2,32,1,2048]{3,1,2,0:T(8,128)S(1)} collective-permute-done((f32[2,32,1,2048]{3,1,2,0:T(8,128)S(1)}, f32[2,32,1,2048]{3,1,2,0:T(8,128)S(1)}, u32[]{:S(2)}, u32[]{:S(2)}) %collective-permute-start.2) | collective-permute-done | bytes 524320 | tf_op jit(solution)/shard_map/ppermute | solution.py:23
  60.3 4.1 %collective-permute-done.3 = f32[2,32,1,2048]{3,1,2,0:T(8,128)S(1)} collective-permute-done((f32[2,32,1,2048]{3,1,2,0:T(8,128)S(1)}, f32[2,32,1,2048]{3,1,2,0:T(8,128)S(1)}, u32[]{:S(2)}, u32[]{:S(2)}) %collective-permute-start.3) | collective-permute-done | bytes 524320 | tf_op jit(solution)/shard_map/ppermute | solution.py:21
  68.0 6.0 %collective-permute-start.5 = (f32[2,32,1,2048]{3,1,2,0:T(8,128)S(1)}, f32[2,32,1,2048]{3,1,2,0:T(8,128)S(1)}, u32[]{:S(2)}, u32[]{:S(2)}) collective-permute-start(f32[2,32,1,2048]{3,1,2,0:T(8,128)S(1)} %get-tuple-element.31), channel_id=1, source_target_pairs={{0,4},{4,8},{8,12},{12,16},{16,20},{20,24},{24,28},{28,32},{32,36}... | collective-permute-start | bytes 1572872 | tf_op jit(solution)/shard_map/ppermute | solution.py:21
  74.8 15.9 %collective-permute-done.4 = f32[2,32,1,2048]{3,1,2,0:T(8,128)S(1)} collective-permute-done((f32[2,32,1,2048]{3,1,2,0:T(8,128)S(1)}, f32[2,32,1,2048]{3,1,2,0:T(8,128)S(1)}, u32[]{:S(2)}, u32[]{:S(2)}) %collective-permute-start.4) | collective-permute-done | bytes 524320 | tf_op jit(solution)/shard_map/ppermute | solution.py:23
  90.7 4.1 %collective-permute-done.5 = f32[2,32,1,2048]{3,1,2,0:T(8,128)S(1)} collective-permute-done((f32[2,32,1,2048]{3,1,2,0:T(8,128)S(1)}, f32[2,32,1,2048]{3,1,2,0:T(8,128)S(1)}, u32[]{:S(2)}, u32[]{:S(2)}) %collective-permute-start.5) | collective-permute-done | bytes 524320 | tf_op jit(solution)/shard_map/ppermute | solution.py:21
  98.3 6.2 %collective-permute-start.7 = (f32[2,32,1,2048]{3,1,2,0:T(8,128)S(1)}, f32[2,32,1,2048]{3,1,2,0:T(8,128)S(1)}, u32[]{:S(2)}, u32[]{:S(2)}) collective-permute-start(f32[2,32,1,2048]{3,1,2,0:T(8,128)S(1)} %get-tuple-element.27), channel_id=1, source_target_pairs={{0,4},{4,8},{8,12},{12,16},{16,20},{20,24},{24,28},{28,32},{32,36}... | collective-permute-start | bytes 1572872 | tf_op jit(solution)/shard_map/ppermute | solution.py:21
  105.3 15.7 %collective-permute-done.6 = f32[2,32,1,2048]{3,1,2,0:T(8,128)S(1)} collective-permute-done((f32[2,32,1,2048]{3,1,2,0:T(8,128)S(1)}, f32[2,32,1,2048]{3,1,2,0:T(8,128)S(1)}, u32[]{:S(2)}, u32[]{:S(2)}) %collective-permute-start.6) | collective-permute-done | bytes 524320 | tf_op jit(solution)/shard_map/ppermute | solution.py:23
  121.0 4.1 %collective-permute-done.7 = f32[2,32,1,2048]{3,1,2,0:T(8,128)S(1)} collective-permute-done((f32[2,32,1,2048]{3,1,2,0:T(8,128)S(1)}, f32[2,32,1,2048]{3,1,2,0:T(8,128)S(1)}, u32[]{:S(2)}, u32[]{:S(2)}) %collective-permute-start.7) | collective-permute-done | bytes 524320 | tf_op jit(solution)/shard_map/ppermute | solution.py:21
  126.9 5.9 %copy.72 = f32[2,32,4,2048]{1,2,0,3:T(4,128)} copy(f32[2,32,4,2048]{3,1,2,0:T(8,128)S(1)} %pad_maximum_fusion.20) | data formatting | bytes 4194304 | tf_op jit(solution)/shard_map/stack | solution.py:53
  132.8 8.5 %reshape.83 = f32[4,1,131072]{2,1,0:T(1,128)} reshape(f32[2048,2,4,32]{3,2,1,0:T(4,128)} %bitcast.84) | data formatting | bytes 4194304
  141.2 3.6 %all-to-all-start = ((f32[4,1,131072]{2,1,0:T(1,128)}), f32[4,1,131072]{2,1,0:T(1,128)S(1)}, u32[]{:S(2)}, u32[]{:S(2)}) async-start(f32[4,1,131072]{2,1,0:T(1,128)} %reshape.83), calls=%async_computation | async-start | bytes 4194304 | tf_op jit(solution)/shard_map/all_to_all | solution.py:93
  145.2 26.9 %all-to-all-done = f32[4,1,131072]{2,1,0:T(1,128)S(1)} async-done(((f32[4,1,131072]{2,1,0:T(1,128)}), f32[4,1,131072]{2,1,0:T(1,128)S(1)}, u32[]{:S(2)}, u32[]{:S(2)}) %all-to-all-start) | async-done | bytes 2097184 | tf_op jit(solution)/shard_map/all_to_all | solution.py:93
  173.9 7.7 %reduce = f32[4,131072]{1,0:T(4,128)S(1)} reduce(f32[4,1,131072]{2,1,0:T(1,128)} %copy-done.1, f32[]{:T(128)} %broadcast.200), dimensions={1}, to_apply=%all_to_all.22.reduce_sub_computation | reduce | bytes 4194308 | tf_op jit(solution)/shard_map/all_to_all | solution.py:93
  181.6 7.8 %reshape.84 = f32[2048,2,4,32]{3,2,1,0:T(4,128)} reshape(f32[4,131072]{1,0:T(4,128)S(1)} %reduce) | data formatting | bytes 4194304
  189.4 6.9 %copy.73 = f32[2,32,4,4,512]{4,1,3,2,0:T(8,128)S(1)} copy(f32[2,32,4,4,512]{1,2,0,4,3:T(4,128)} %bitcast.85) | data formatting | bytes 4194304 | tf_op jit(solution)/shard_map/all_to_all | solution.py:93
  201.5 2.1 copy.76
  203.6 30.8 %all_to_all.30 = f32[2,128,4,512]{3,2,0,1:T(4,128)S(1)} all-to-all(f32[2,128,4,512]{3,2,0,1:T(4,128)} %copy.76), channel_id=1, replica_groups=mesh['lat'=64,'depth'=4] {'depth'}, dimensions={1} | all-to-all | bytes 4194304 | tf_op jit(solution)/shard_map/all_to_all | solution.py:100
  (53 shorter events, 29.1 us)
Async XLA Ops:
  0.6 197.0 %copy-start = (f32[128,128]{1,0:T(8,128)S(1)}, f32[128,128]{1,0:T(8,128)}, u32[]{:S(2)}) copy-start(f32[128,128]{1,0:T(8,128)} %param.13) | copy-start | bytes 196612
  3.5 24.8 %collective-permute-start = (f32[2,32,1,2048]{3,1,2,0:T(8,128)S(1)}, f32[2,32,1,2048]{3,1,2,0:T(8,128)S(1)}, u32[]{:S(2)}, u32[]{:S(2)}) collective-permute-start(f32[2,32,1,2048]{3,1,2,0:T(8,128)S(1)} %get-tuple-element.38), channel_id=1, source_target_pairs={{4,0},{8,4},{12,8},{16,12},{20,16},{24,20},{28,24},{32,28},{36,32}... | collective-permute-start | bytes 1572872 | tf_op jit(solution)/shard_map/ppermute | solution.py:23
  6.0 6.5 %copy-start.5 = (s32[4,2048]{1,0:T(4,128)S(1)}, s32[4,2048]{1,0:T(4,128)}, u32[]{:S(2)}) copy-start(s32[4,2048]{1,0:T(4,128)} %param.9) | copy-start | bytes 98308
  6.0 6.4 %copy-start.6 = (f32[12]{0:T(128)S(1)}, f32[12]{0:T(128)}, u32[]{:S(2)}) copy-start(f32[12]{0:T(128)} %param.10) | copy-start | bytes 148
  6.0 6.4 %copy-start.7 = (f32[12]{0:T(128)S(1)}, f32[12]{0:T(128)}, u32[]{:S(2)}) copy-start(f32[12]{0:T(128)} %param.11) | copy-start | bytes 148
  6.0 26.4 %collective-permute-start.1 = (f32[2,32,1,2048]{3,1,2,0:T(8,128)S(1)}, f32[2,32,1,2048]{3,1,2,0:T(8,128)S(1)}, u32[]{:S(2)}, u32[]{:S(2)}) collective-permute-start(f32[2,32,1,2048]{3,1,2,0:T(8,128)S(1)} %get-tuple-element.39), channel_id=1, source_target_pairs={{0,4},{4,8},{8,12},{12,16},{16,20},{20,24},{24,28},{28,32},{32,36}... | collective-permute-start | bytes 1572872 | tf_op jit(solution)/shard_map/ppermute | solution.py:21
  32.4 1.2 copy-start.2
  32.4 1.5 copy-start.3
  35.5 24.8 %collective-permute-start.2 = (f32[2,32,1,2048]{3,1,2,0:T(8,128)S(1)}, f32[2,32,1,2048]{3,1,2,0:T(8,128)S(1)}, u32[]{:S(2)}, u32[]{:S(2)}) collective-permute-start(f32[2,32,1,2048]{3,1,2,0:T(8,128)S(1)} %get-tuple-element.34), channel_id=1, source_target_pairs={{4,0},{8,4},{12,8},{16,12},{20,16},{24,20},{28,24},{32,28},{36,32}... | collective-permute-start | bytes 1572872 | tf_op jit(solution)/shard_map/ppermute | solution.py:23
  37.4 27.0 %collective-permute-start.3 = (f32[2,32,1,2048]{3,1,2,0:T(8,128)S(1)}, f32[2,32,1,2048]{3,1,2,0:T(8,128)S(1)}, u32[]{:S(2)}, u32[]{:S(2)}) collective-permute-start(f32[2,32,1,2048]{3,1,2,0:T(8,128)S(1)} %get-tuple-element.35), channel_id=1, source_target_pairs={{0,4},{4,8},{8,12},{12,16},{16,20},{20,24},{24,28},{28,32},{32,36}... | collective-permute-start | bytes 1572872 | tf_op jit(solution)/shard_map/ppermute | solution.py:21
  66.0 24.6 %collective-permute-start.4 = (f32[2,32,1,2048]{3,1,2,0:T(8,128)S(1)}, f32[2,32,1,2048]{3,1,2,0:T(8,128)S(1)}, u32[]{:S(2)}, u32[]{:S(2)}) collective-permute-start(f32[2,32,1,2048]{3,1,2,0:T(8,128)S(1)} %get-tuple-element.30), channel_id=1, source_target_pairs={{4,0},{8,4},{12,8},{16,12},{20,16},{24,20},{28,24},{32,28},{36,32}... | collective-permute-start | bytes 1572872 | tf_op jit(solution)/shard_map/ppermute | solution.py:23
  68.0 26.8 %collective-permute-start.5 = (f32[2,32,1,2048]{3,1,2,0:T(8,128)S(1)}, f32[2,32,1,2048]{3,1,2,0:T(8,128)S(1)}, u32[]{:S(2)}, u32[]{:S(2)}) collective-permute-start(f32[2,32,1,2048]{3,1,2,0:T(8,128)S(1)} %get-tuple-element.31), channel_id=1, source_target_pairs={{0,4},{4,8},{8,12},{12,16},{16,20},{20,24},{24,28},{28,32},{32,36}... | collective-permute-start | bytes 1572872 | tf_op jit(solution)/shard_map/ppermute | solution.py:21
  96.4 24.6 %collective-permute-start.6 = (f32[2,32,1,2048]{3,1,2,0:T(8,128)S(1)}, f32[2,32,1,2048]{3,1,2,0:T(8,128)S(1)}, u32[]{:S(2)}, u32[]{:S(2)}) collective-permute-start(f32[2,32,1,2048]{3,1,2,0:T(8,128)S(1)} %get-tuple-element.26), channel_id=1, source_target_pairs={{4,0},{8,4},{12,8},{16,12},{20,16},{24,20},{28,24},{32,28},{36,32}... | collective-permute-start | bytes 1572872 | tf_op jit(solution)/shard_map/ppermute | solution.py:23
  98.3 26.8 %collective-permute-start.7 = (f32[2,32,1,2048]{3,1,2,0:T(8,128)S(1)}, f32[2,32,1,2048]{3,1,2,0:T(8,128)S(1)}, u32[]{:S(2)}, u32[]{:S(2)}) collective-permute-start(f32[2,32,1,2048]{3,1,2,0:T(8,128)S(1)} %get-tuple-element.27), channel_id=1, source_target_pairs={{0,4},{4,8},{8,12},{12,16},{16,20},{20,24},{24,28},{28,32},{32,36}... | collective-permute-start | bytes 1572872 | tf_op jit(solution)/shard_map/ppermute | solution.py:21
  141.2 30.8 %all-to-all-start = ((f32[4,1,131072]{2,1,0:T(1,128)}), f32[4,1,131072]{2,1,0:T(1,128)S(1)}, u32[]{:S(2)}, u32[]{:S(2)}) async-start(f32[4,1,131072]{2,1,0:T(1,128)} %reshape.83), calls=%async_computation | async-start | bytes 4194304 | tf_op jit(solution)/shard_map/all_to_all | solution.py:93
  172.0 1.3 copy-start.1
  197.7 1.8 copy-start.4
where the time goes:
time: 242 us; the launch traced here: 241 us
  waiting for transfers between devices  107 us (44%)
  local copies, waits for them, and re-layouts  43.1 us (18%)
  starting transfers between devices  35.7 us (15%)
  blocking collectives  30.8 us (13%)
  other arithmetic  19.1 us (8%)
  matrix products  4.72 us (2%)
    ppermute x4, waiting for transfers between devices, extended(): lax.ppermute(head, axis, [((i + 1) % count, i) for i in range(ends)])  63.2 us
    all_to_all x1, blocking collectives, per_device(): lax.all_to_all(solved, 'depth', split_axis=1, concat_axis=3, tiled=True)  30.8 us
    all_to_all x1, waiting for transfers between devices, per_device(): lax.all_to_all(profile_snapshot, 'depth', split_axis=3, concat_axis=1, ti...  26.9 us
    ppermute x4, starting transfers between devices, extended(): lax.ppermute(tail, axis, [(i, (i + 1) % count) for i in range(ends)])  23.9 us
    unnamed x22, local copies, waits for them, and re-layouts  23.2 us
    ppermute x4, waiting for transfers between devices, extended(): lax.ppermute(tail, axis, [(i, (i + 1) % count) for i in range(ends)])  16.4 us
    ppermute x4, starting transfers between devices, extended(): lax.ppermute(head, axis, [((i + 1) % count, i) for i in range(ends)])  8.2 us
    all_to_all x1, other arithmetic, per_device(): lax.all_to_all(profile_snapshot, 'depth', split_axis=3, concat_axis=1, ti...  7.72 us
  transfers between devices with their start and end apart: 9, of which 9 were waited for; matrix products, arithmetic and copies ran while one was open for 1% of the time, Pallas kernels for 0%

commit v1 on v0

v1 whole, which is shorter than its diff:
```python
import functools

import jax
import jax.numpy as jnp
import numpy as np
from jax import lax
from jax.experimental import pallas as pl
from jax.experimental.pallas import tpu as pltpu
from jax.sharding import PartitionSpec as P

MESH = pl.DeviceIdType.MESH
LEVELS = 128
CLASSES = 12
LSUB = 4
CHUNKS = 2
LANES = 128
SLAB = 32
PIECE = 272
OFFSETS = [(h, l, c) for h in (0, 1) for l in (0, 1) for c in (0, 1)]


def scaled_derivative():
    f32 = np.float32
    index = np.arange(LEVELS).astype(f32)
    nodes = np.cos(f32(np.pi) * index / f32(LEVELS - 1)).astype(f32)
    ends = np.where((index == 0) | (index == LEVELS - 1), 2.0, 1.0)
    signs = np.where(np.arange(LEVELS) % 2 == 0, 1.0, -1.0)
    weight = (ends * signs).astype(f32)
    diagonal = np.eye(LEVELS, dtype=bool)
    spread = nodes[:, None] - nodes[None, :]
    off = weight[:, None] / weight[None, :] / np.where(diagonal, f32(1), spread)
    off = np.where(diagonal, f32(0), off)
    deriv = off - np.diag(np.sum(off, axis=1))
    scale = (f32(1) - nodes * nodes) / f32(LEVELS)
    return (scale[:, None] * deriv).astype(f32)


def flip(value, bit):
    return 1 - value if bit else value


def kernel(
    pairs,
    heat_ref, wet_ref, label_ref, spread_ref, factor_ref, thermal_ref, water_ref, deriv_ref,
    heat_out, wet_out,
    slab, block, piece, kloc, ksend, kgot, coef, kmid, state, solved, result, mats,
    load_sem, own_sem, xsend, xrecv, zsend, zrecv, kown_sem, kx_sem, kz_sem, kzrecv, rown_sem, rsend, rrecv, store_sem,
):
    my_lat = lax.axis_index("lat")
    my_d = lax.axis_index("depth")
    pair, lo = my_lat // 2, my_lat % 2
    hi, core = my_d // 2, my_d % 2
    me = lo * 4 + my_d
    has_before, has_after = pair > 0, pair < pairs - 1

    def place(o):
        h, l, c = o
        lo2 = flip(lo, l)
        d2 = flip(hi, h) * 2 + flip(core, c)
        return lo2, d2, (pair * 2 + lo2, d2)

    loads = []
    for f, src in enumerate((heat_ref, wet_ref)):
        for r in range(4):
            loads.append(pltpu.make_async_copy(src.at[:, r, :], slab.at[f, r], load_sem.at[f * 4 + r]))
    for cp in loads:
        cp.start()

    barrier = pltpu.get_barrier_semaphore()
    for o in OFFSETS[1:]:
        pl.semaphore_signal(barrier, inc=1, device_id=place(o)[2], device_id_type=MESH)

    @pl.when(has_before)
    def _():
        pl.semaphore_signal(barrier, inc=1, device_id=(my_lat - 2, my_d), device_id_type=MESH)

    @pl.when(has_after)
    def _():
        pl.semaphore_signal(barrier, inc=1, device_id=(my_lat + 2, my_d), device_id_type=MESH)

    lane = lax.broadcasted_iota(jnp.int32, (8, LANES), 1)
    right, left = lane < 4, lane >= LANES - 4

    kloc[0] = jnp.zeros((8, LANES), jnp.float32)
    kloc[17] = jnp.zeros((8, LANES), jnp.float32)
    for t in range(16):
        label = label_ref[:, t * LANES:(t + 1) * LANES]
        kh = jnp.zeros((4, LANES), jnp.float32)
        km = jnp.zeros((4, LANES), jnp.float32)
        for n in range(CLASSES):
            kh = jnp.where(label == n, spread_ref[n], kh)
            km = jnp.where(label == n, factor_ref[n], km)
        kloc[t + 1, 0:4] = kh
        kloc[t + 1, 4:8] = km

    def kblock(t):
        main = kloc[t + 1]
        edge = jnp.where(right, kloc[t + 2], jnp.where(left, kloc[t], 0.0))
        return main, edge

    partner = (0, 1, 0)
    plo, pd, pdev = place(partner)
    for k in range(CHUNKS):
        main, edge = kblock(k * 8 + plo * 4 + pd)
        ksend[k, 0] = main
        ksend[k, 1] = edge
        main, edge = kblock(k * 8 + me)
        kgot[1 + lo, k, 0] = main
        kgot[1 + lo, k, 1] = edge

    @pl.when(jnp.logical_not(has_before))
    def _():
        kgot[0] = jnp.zeros((CHUNKS, 2, 8, LANES), jnp.float32)

        @pl.loop(0, CHUNKS * 4)
        def _(i):
            piece[i // 4, 0, i % 4] = jnp.zeros((PIECE, LANES), jnp.float32)

    @pl.when(jnp.logical_not(has_after))
    def _():
        kgot[3] = jnp.zeros((CHUNKS, 2, 8, LANES), jnp.float32)

        @pl.loop(0, CHUNKS * 4)
        def _(i):
            piece[i // 4, 3, i % 4] = jnp.zeros((PIECE, LANES), jnp.float32)

    for cp in loads:
        cp.wait()

    def build(k):
        @pl.loop(0, 8)
        def _(j):
            t = k * 8 + j
            here = pl.multiple_of(t * LANES, LANES)
            before = pl.multiple_of(jnp.maximum(t - 1, 0) * LANES, LANES)
            after = pl.multiple_of(jnp.minimum(t + 1, 15) * LANES, LANES)
            keep_left = jnp.logical_and(left, t > 0)
            keep_right = jnp.logical_and(right, t < 15)
            for f in range(2):
                packed = jnp.zeros((8, LANES), jnp.float32)
                for r in range(4):
                    for q in range(4):
                        g = r * 4 + q
                        rows = pl.ds(q * 8, 8)
                        block[t, pl.ds((f * 16 + g) * 8, 8), :] = slab[f, r, rows, pl.ds(here, LANES)]
                        edge = jnp.where(
                            keep_right,
                            slab[f, r, rows, pl.ds(after, LANES)],
                            jnp.where(keep_left, slab[f, r, rows, pl.ds(before, LANES)], 0.0),
                        )
                        packed = packed + (pltpu.roll(edge, 8 * g, 1) if g else edge)
                block[t, pl.ds(256 + f * 8, 8), :] = packed

    def x_copy(k, o):
        lo2, d2, dev = place(o)
        n = OFFSETS.index(o)
        return pltpu.make_async_remote_copy(
            src_ref=block.at[k * 8 + lo2 * 4 + d2],
            dst_ref=piece.at[k, 1 + lo, o[0] * 2 + o[2]],
            send_sem=xsend.at[k, n],
            recv_sem=xrecv.at[k, n],
            device_id=dev,
            device_id_type=MESH,
        )

    def x_arrival(k, o):
        lo2, d2, dev = place(o)
        n = OFFSETS.index(o)
        return pltpu.make_async_remote_copy(
            src_ref=block.at[k * 8 + lo2 * 4 + d2],
            dst_ref=piece.at[k, 1 + lo2, o[0] * 2 + o[2]],
            send_sem=xsend.at[k, n],
            recv_sem=xrecv.at[k, n],
            device_id=dev,
            device_id_type=MESH,
        )

    def own_copy(k):
        return pltpu.make_async_copy(block.at[k * 8 + me], piece.at[k, 1 + lo, 0], own_sem.at[k])

    def forward_copy(k, o, s):
        n = OFFSETS.index(o)
        q = o[0] * 2 + o[2]
        return pltpu.make_async_remote_copy(
            src_ref=piece.at[k, 1 + s, q],
            dst_ref=piece.at[k, 3 if s == 0 else 0, q],
            send_sem=zsend.at[k, n],
            recv_sem=zrecv.at[k, q, s],
            device_id=(my_lat - 2 if s == 0 else my_lat + 2, my_d),
            device_id_type=MESH,
        )

    def forward(k, o, act):
        lo2 = flip(lo, o[1])

        @pl.when(jnp.logical_and(lo2 == 0, has_before))
        def _():
            act(forward_copy(k, o, 0))

        @pl.when(jnp.logical_and(lo2 == 1, has_after))
        def _():
            act(forward_copy(k, o, 1))

    def halo_wait(k, q):
        o = (q // 2, 0, q % 2)

        @pl.when(has_after)
        def _():
            forward_copy(k, o, 0).wait_recv()

        @pl.when(has_before)
        def _():
            forward_copy(k, o, 1).wait_recv()

    def k_forward(s, act):
        @pl.when(has_before if s == 0 else has_after)
        def _():
            act(
                pltpu.make_async_remote_copy(
                    src_ref=kgot.at[1 + s],
                    dst_ref=kgot.at[3 if s == 0 else 0],
                    send_sem=kz_sem.at[s],
                    recv_sem=kzrecv.at[s],
                    device_id=(my_lat - 2 if s == 0 else my_lat + 2, my_d),
                    device_id_type=MESH,
                )
            )

    def k_copy(strip):
        return pltpu.make_async_remote_copy(
            src_ref=ksend,
            dst_ref=kgot.at[1 + strip],
            send_sem=kx_sem.at[0],
            recv_sem=kx_sem.at[1],
            device_id=pdev,
            device_id_type=MESH,
        )

    near = [(0, 1, 0), (0, 1, 1), (1, 1, 0), (1, 1, 1)]
    far = [(1, 0, 0), (1, 0, 1)]
    sibling = (0, 0, 1)
    remote = [sibling] + near + far

    build(0)
    inner = jnp.logical_and(has_before, has_after)

    @pl.when(inner)
    def _():
        pl.semaphore_wait(barrier, 9)

    @pl.when(jnp.logical_not(inner))
    def _():
        pl.semaphore_wait(barrier, 8 if pairs > 1 else 7)

    start = lambda cp: cp.start()
    k_copy(lo).start()
    for o in remote:
        x_copy(0, o).start()
    own_copy(0).start()
    build(1)
    own_copy(0).wait()
    forward(0, (0, 0, 0), start)
    own_copy(1).start()

    highest = lax.Precision.HIGHEST
    mats[0, :, 0:LEVELS] = thermal_ref[...]
    mats[1, :, 0:LEVELS] = water_ref[...]
    mats[0, :, LEVELS:] = -0.25 * jnp.dot(thermal_ref[...], deriv_ref[...], precision=highest, preferred_element_type=jnp.float32)
    mats[1, :, LEVELS:] = 0.5 * jnp.dot(water_ref[...], deriv_ref[...], precision=highest, preferred_element_type=jnp.float32)

    k_copy(1 - lo).wait_recv()
    k_forward(0, start)
    k_forward(1, start)

    def arrive(k, o):
        x_arrival(k, o).wait_recv()
        forward(k, o, start)

    arrive(0, sibling)
    own_copy(1).wait()

    def k_received():
        @pl.when(has_after)
        def _():
            pltpu.make_async_remote_copy(
                src_ref=kgot.at[1], dst_ref=kgot.at[3], send_sem=kz_sem.at[0], recv_sem=kzrecv.at[0],
                device_id=(my_lat - 2, my_d), device_id_type=MESH,
            ).wait_recv()

        @pl.when(has_before)
        def _():
            pltpu.make_async_remote_copy(
                src_ref=kgot.at[2], dst_ref=kgot.at[0], send_sem=kz_sem.at[1], recv_sem=kzrecv.at[1],
                device_id=(my_lat + 2, my_d), device_id_type=MESH,
            ).wait_recv()

        for k in range(CHUNKS):
            for r in range(16):
                for part in range(2):
                    cols = slice(part * LANES, (part + 1) * LANES)
                    kh = jnp.broadcast_to(kgot[r // 4, k, part, r % 4:r % 4 + 1, :], (8, LANES))
                    km = jnp.broadcast_to(kgot[r // 4, k, part, 4 + r % 4:5 + r % 4, :], (8, LANES))
                    coef[k, 0, r, :, cols] = 0.375 * kh
                    coef[k, 1, r, :, cols] = 0.125 * kh
                    coef[k, 2, r, :, cols] = 0.25 * km
                    if part == 0 and 4 <= r < 12:
                        half = slice(((r - 4) % 2) * LANES, ((r - 4) % 2 + 1) * LANES)
                        kmid[k, (r - 4) // 2, :, half] = km

    inside = jnp.logical_or(right, left)

    def stencil(k, q):
        d = flip(hi, q // 2) * 2 + flip(core, q % 2)

        @pl.loop(0, 4)
        def _(tile):
            level = pl.multiple_of(d * SLAB + tile * 8, 8)

            def load(r, f):
                row = r % 4
                main = piece[k, r // 4, q, pl.ds(pl.multiple_of((f * 16 + row * 4 + tile) * 8, 8), 8), :]
                packed = piece[k, r // 4, q, pl.ds(256 + f * 8, 8), :]
                shift = lax.rem(LANES - 8 * (row * 4 + tile), LANES)
                edge = jnp.where(inside, pltpu.roll(packed, shift, 1), 0.0)
                return jnp.concatenate([main, edge], axis=1)

            def lap(rows, r):
                centre = rows[r]
                east = pltpu.roll(centre, 2 * LANES - 1, 1)
                west = pltpu.roll(centre, 1, 1)
                return rows[r + 1] + rows[r - 1] + east + west - 4.0 * centre

            heat = [{} for _ in range(LSUB + 1)]
            wet = [{} for _ in range(LSUB + 1)]
            for front in range(16):
                heat[0][front] = load(front, 0)
                wet[0][front] = load(front, 1)
                for t in range(1, LSUB + 1):
                    r = front - t
                    if r < t or r > 15 - t:
                        continue
                    h, w = heat[t - 1][r], wet[t - 1][r]
                    factor = coef[k, 0, r] - coef[k, 1, r] / (1.0 + w * w)
                    heat[t][r] = h + factor * lap(heat[t - 1], r)
                    wet[t][r] = w + coef[k, 2, r] * lap(wet[t - 1], r)
                    if t == LSUB:
                        half = slice(((r - 4) % 2) * LANES, ((r - 4) % 2 + 1) * LANES)
                        state[k, 0, (r - 4) // 2, pl.ds(level, 8), half] = heat[t][r][:, :LANES]
                        state[k, 1, (r - 4) // 2, pl.ds(level, 8), half] = wet[t][r][:, :LANES]

    def r_copy(k, half, o):
        lo2, d2, dev = place(o)
        n = OFFSETS.index(o)
        return pltpu.make_async_remote_copy(
            src_ref=solved.at[k, :, pl.ds(lo2 * 4 + half * 2, 2), pl.ds(pl.multiple_of(d2 * SLAB, SLAB), SLAB), :],
            dst_ref=result.at[:, pl.ds(half * 2, 2), :, pl.ds(pl.multiple_of((k * 8 + me) * LANES, LANES), LANES)],
            send_sem=rsend.at[k, half, n],
            recv_sem=rrecv.at[k, half, n],
            device_id=dev,
            device_id_type=MESH,
        )

    def r_arrival(k, half, o):
        lo2, d2, dev = place(o)
        n = OFFSETS.index(o)
        src = (k * 8 + lo2 * 4 + d2) * LANES
        return pltpu.make_async_remote_copy(
            src_ref=solved.at[k, :, pl.ds(lo2 * 4 + half * 2, 2), pl.ds(pl.multiple_of(d2 * SLAB, SLAB), SLAB), :],
            dst_ref=result.at[:, pl.ds(half * 2, 2), :, pl.ds(pl.multiple_of(src, LANES), LANES)],
            send_sem=rsend.at[k, half, n],
            recv_sem=rrecv.at[k, half, n],
            device_id=dev,
            device_id_type=MESH,
        )

    def r_own(k, half):
        return pltpu.make_async_copy(
            solved.at[k, :, pl.ds(lo * 4 + half * 2, 2), pl.ds(pl.multiple_of(my_d * SLAB, SLAB), SLAB), :],
            result.at[:, pl.ds(half * 2, 2), :, pl.ds(pl.multiple_of((k * 8 + me) * LANES, LANES), LANES)],
            rown_sem.at[k, half],
        )

    def solve(k):
        for half in range(2):
            for l in (1, 0):
                rp = flip(lo, l) * 2 + half
                h = state[k, 0, rp]
                w = state[k, 1, rp]
                kw = w * kmid[k, rp, 0:1, :]
                temp = jnp.dot(mats[0], jnp.concatenate([h, kw], axis=0), precision=highest, preferred_element_type=jnp.float32)
                moist = jnp.dot(mats[1], jnp.concatenate([w, kw], axis=0), precision=highest, preferred_element_type=jnp.float32)
                for f, out in enumerate((temp, moist)):
                    solved[k, f, rp * 2] = out[:, :LANES]
                    solved[k, f, rp * 2 + 1] = out[:, LANES:]
                for o in [(1, l, 0), (1, l, 1), (0, l, 0), (0, l, 1)]:
                    if o == (0, 0, 0):
                        r_own(k, half).start()
                    else:
                        r_copy(k, half, o).start()

    for o in near:
        arrive(0, o)
    for o in far:
        arrive(0, o)
    for o in remote:
        x_copy(1, o).start()
    forward(1, (0, 0, 0), start)
    k_received()
    arrive(1, sibling)
    halo_wait(0, 0)
    stencil(0, 0)
    halo_wait(0, 1)
    stencil(0, 1)
    halo_wait(0, 2)
    stencil(0, 2)
    for o in near:
        arrive(1, o)
    halo_wait(0, 3)
    stencil(0, 3)
    solve(0)
    for o in far:
        arrive(1, o)
    for q in range(4):
        halo_wait(1, q)
        stencil(1, q)
    solve(1)

    def store(k):
        cols = pl.ds(k * 8 * LANES, 8 * LANES)
        copies = []
        for f, out in enumerate((heat_out, wet_out)):
            for r in range(4):
                copies.append(pltpu.make_async_copy(result.at[f, r, :, cols], out.at[:, r, cols], store_sem.at[k, f * 4 + r]))
        return copies

    for k in range(CHUNKS):
        for half in range(2):
            r_own(k, half).wait()
            for o in remote:
                r_arrival(k, half, o).wait_recv()
        for cp in store(k):
            cp.start()

    k_copy(lo).wait_send()
    k_forward(0, lambda cp: cp.wait_send())
    k_forward(1, lambda cp: cp.wait_send())
    for k in range(CHUNKS):
        for o in remote:
            x_copy(k, o).wait_send()
        for o in OFFSETS:
            forward(k, o, lambda cp: cp.wait_send())
        for half in range(2):
            for o in remote:
                r_copy(k, half, o).wait_send()
        for cp in store(k):
            cp.wait()


def solution(mesh):
    pairs = mesh.shape["lat"] // 2
    deriv = scaled_derivative()

    def per_device(heat, wet, label, spread, factor, thermal, water):
        any_spec = pl.BlockSpec(memory_space=pl.ANY)
        vmem = pl.BlockSpec(memory_space=pltpu.VMEM)
        smem = pl.BlockSpec(memory_space=pltpu.SMEM)
        dma = pltpu.SemaphoreType.DMA
        f32 = jnp.float32
        out = jax.ShapeDtypeStruct(heat.shape, f32)
        return pl.pallas_call(
            functools.partial(kernel, pairs),
            out_shape=(out, out),
            in_specs=[any_spec, any_spec, vmem, smem, smem, vmem, vmem, vmem],
            out_specs=(any_spec, any_spec),
            scratch_shapes=[
                pltpu.VMEM((2, 4, SLAB, 16 * LANES), f32),
                pltpu.VMEM((16, PIECE, LANES), f32),
                pltpu.VMEM((CHUNKS, 4, 4, PIECE, LANES), f32),
                pltpu.VMEM((18, 8, LANES), f32),
                pltpu.VMEM((CHUNKS, 2, 8, LANES), f32),
                pltpu.VMEM((4, CHUNKS, 2, 8, LANES), f32),
                pltpu.VMEM((CHUNKS, 3, 16, 8, 2 * LANES), f32),
                pltpu.VMEM((CHUNKS, 4, 8, 2 * LANES), f32),
                pltpu.VMEM((CHUNKS, 2, 4, LEVELS, 2 * LANES), f32),
                pltpu.VMEM((CHUNKS, 2, 8, LEVELS, LANES), f32),
                pltpu.VMEM((2, 4, SLAB, 16 * LANES), f32),
                pltpu.VMEM((2, LEVELS, 2 * LEVELS), f32),
                dma((8,)),
                dma((CHUNKS,)),
                dma((CHUNKS, 8)),
                dma((CHUNKS, 8)),
                dma((CHUNKS, 8)),
                dma((CHUNKS, 4, 2)),
                dma((1,)),
                dma((2,)),
                dma((2,)),
                dma((2,)),
                dma((CHUNKS, 2)),
                dma((CHUNKS, 2, 8)),
                dma((CHUNKS, 2, 8)),
                dma((CHUNKS, 8)),
            ],
            compiler_params=pltpu.CompilerParams(
                collective_id=0, has_side_effects=True, vmem_limit_bytes=48 << 20
            ),
        )(heat, wet, label, spread, factor, thermal, water, jnp.asarray(deriv))

    return jax.shard_map(
        per_device,
        mesh=mesh,
        in_specs=(
            P("depth", "lat", None),
            P("depth", "lat", None),
            P("lat", None),
            P(),
            P(),
            P(),
            P(),
        ),
        out_specs=(P("depth", "lat", None), P("depth", "lat", None)),
        check_vma=False,
    )
```

time: 242 us -> 79.5 us (0.33)
  the two profiles are of different devices: /device:TPU:98 before, /device:TPU:25 now
where the time goes in v1:
time: 79.5 us; the launch traced here: 78.1 us
  Pallas kernels  68.4 us (86%)
  local copies, waits for them, and re-layouts  8.97 us (11%)
    pallas_call x1, Pallas kernels, per_device(): pl.pallas_call(functools.partial(kernel, pairs), out_shape=(out, out), in...  68.4 us
    unnamed x18, local copies, waits for them, and re-layouts  8.97 us

profile of v1, /device:TPU:25, one launch (start us, length us, event | category | flops | bytes accessed | tf_op | source)
XLA Modules:
  0.0 78.1 jit_solution(13486186771119819191)
XLA Ops:
  0.6 0.0 copy-start
  0.6 1.2 %copy-done = f32[32,4,2048]{2,1,0:T(4,128)S(1)} copy-done((f32[32,4,2048]{2,1,0:T(4,128)S(1)}, f32[32,4,2048]{2,1,0:T(4,128)}, u32[]{:S(2)}) %copy-start) | copy-done | bytes 1048600
  1.9 0.0 copy-start.1
  1.9 1.2 %copy-done.1 = f32[32,4,2048]{2,1,0:T(4,128)S(1)} copy-done((f32[32,4,2048]{2,1,0:T(4,128)S(1)}, f32[32,4,2048]{2,1,0:T(4,128)}, u32[]{:S(2)}) %copy-start.1) | copy-done | bytes 1048600
  3.1 0.0 copy-start.2
  3.1 0.8 %copy-done.2 = f32[128,128]{1,0:T(8,128)S(1)} copy-done((f32[128,128]{1,0:T(8,128)S(1)}, f32[128,128]{1,0:T(8,128)}, u32[]{:S(2)}) %copy-start.2) | copy-done | bytes 65560
  3.9 0.0 copy-start.3
  3.9 0.8 %copy-done.3 = f32[128,128]{1,0:T(8,128)S(1)} copy-done((f32[128,128]{1,0:T(8,128)S(1)}, f32[128,128]{1,0:T(8,128)}, u32[]{:S(2)}) %copy-start.3) | copy-done | bytes 65560
  4.8 0.0 copy-start.4
  4.8 0.8 %copy-done.4 = f32[128,128]{1,0:T(8,128)S(1)} copy-done((f32[128,128]{1,0:T(8,128)S(1)}, f32[128,128]{1,0:T(8,128)}, u32[]{:S(2)}) %copy-start.4) | copy-done | bytes 65560
  5.6 0.0 copy-start.5
  5.6 0.8 copy-done.5
  6.4 0.0 copy-start.6
  6.4 0.7 copy-done.6
  7.0 0.0 copy-start.7
  7.0 0.7 copy-done.7
  7.7 68.4 %shard_map.95 = (f32[32,4,2048]{2,1,0:T(4,128)S(1)}, f32[32,4,2048]{2,1,0:T(4,128)S(1)}) custom-call(f32[32,4,2048]{2,1,0:T(4,128)S(1)} %copy-done, f32[32,4,2048]{2,1,0:T(4,128)S(1)} %copy-done.1, s32[4,2048]{1,0:T(4,128)S(1)} %copy-done.5, f32[12]{0:T(128)S(1)} %copy-done.6, f32[12]{0:T(128)S(1)} %copy-done.7, f32[128,128]{1,0:T(8,128)S(1)} %copy-done.2, ...), custom_call_target="tpu_custom_call" | custom-call | tf_op jit(solution)/shard_map/pallas_call | solution.py:470
  76.1 1.0 %copy.12 = f32[32,4,2048]{2,1,0:T(4,128)} copy(f32[32,4,2048]{2,1,0:T(4,128)S(1)} %get-tuple-element.4) | data formatting | bytes 2097152
  77.1 1.0 %copy.13 = f32[32,4,2048]{2,1,0:T(4,128)} copy(f32[32,4,2048]{2,1,0:T(4,128)S(1)} %get-tuple-element.5) | data formatting | bytes 2097152
Async XLA Ops:
  0.6 1.2 %copy-start = (f32[32,4,2048]{2,1,0:T(4,128)S(1)}, f32[32,4,2048]{2,1,0:T(4,128)}, u32[]{:S(2)}) copy-start(f32[32,4,2048]{2,1,0:T(4,128)} %heat_ref.1) | copy-start | bytes 3145732
  1.9 1.2 %copy-start.1 = (f32[32,4,2048]{2,1,0:T(4,128)S(1)}, f32[32,4,2048]{2,1,0:T(4,128)}, u32[]{:S(2)}) copy-start(f32[32,4,2048]{2,1,0:T(4,128)} %wet_ref.1) | copy-start | bytes 3145732
  3.1 0.8 %copy-start.2 = (f32[128,128]{1,0:T(8,128)S(1)}, f32[128,128]{1,0:T(8,128)}, u32[]{:S(2)}) copy-start(f32[128,128]{1,0:T(8,128)} %thermal_ref.1) | copy-start | bytes 196612
  3.9 0.8 %copy-start.3 = (f32[128,128]{1,0:T(8,128)S(1)}, f32[128,128]{1,0:T(8,128)}, u32[]{:S(2)}) copy-start(f32[128,128]{1,0:T(8,128)} %water_ref.1) | copy-start | bytes 196612
  4.8 0.8 %copy-start.4 = (f32[128,128]{1,0:T(8,128)S(1)}, f32[128,128]{1,0:T(8,128)}, u32[]{:S(2)}) copy-start(f32[128,128]{1,0:T(8,128)} %constant.2.clone.deriv_ref) | copy-start | bytes 196612
  5.6 0.8 copy-start.5
  6.4 0.7 copy-start.6
  7.0 0.7 copy-start.7

commit v2 on v1

--- a/solution.py
+++ b/solution.py
@@ -400,11 +400,11 @@
 
     for o in near:
         arrive(0, o)
-    for o in far:
-        arrive(0, o)
     for o in remote:
         x_copy(1, o).start()
     forward(1, (0, 0, 0), start)
+    for o in far:
+        arrive(0, o)
     k_received()
     arrive(1, sibling)
     halo_wait(0, 0)
@@ -503,7 +503,7 @@
             compiler_params=pltpu.CompilerParams(
                 collective_id=0, has_side_effects=True, vmem_limit_bytes=48 << 20
             ),
-        )(heat, wet, label, spread, factor, thermal, water, jnp.asarray(deriv))
+        )(*(pltpu.with_memory_space_constraint(x, pltpu.HBM) for x in (heat, wet, label, spread, factor, thermal, water, jnp.asarray(deriv))))
 
     return jax.shard_map(
         per_device,

time: 79.5 us -> 70.7 us (0.89); the launches traced: 78.1 us -> 70.6 us
  local copies, waits for them, and re-layouts: 8.97 us -> 1.94 us
    unnamed x18 -> x2, local copies, waits for them, and re-layouts: 8.97 us -> 1.94 us
where the time goes in v2:
time: 70.7 us; the launch traced here: 70.6 us
  Pallas kernels  68 us (96%)
  local copies, waits for them, and re-layouts  1.94 us (3%)
    pallas_call x1, Pallas kernels, per_device(): pl.pallas_call(functools.partial(kernel, pairs), out_shape=(out, out), in...  68 us
    unnamed x2, local copies, waits for them, and re-layouts  1.94 us

profile of v2, /device:TPU:25, one launch (start us, length us, event | category | flops | bytes accessed | tf_op | source)
XLA Modules:
  0.0 70.6 jit_solution(10379978420337392498)
XLA Ops:
  0.6 68.0 %shard_map.95 = (f32[32,4,2048]{2,1,0:T(4,128)S(1)}, f32[32,4,2048]{2,1,0:T(4,128)S(1)}) custom-call(f32[32,4,2048]{2,1,0:T(4,128)} %heat_ref.1, f32[32,4,2048]{2,1,0:T(4,128)} %wet_ref.1, s32[4,2048]{1,0:T(4,128)} %label_ref.1, f32[12]{0:T(128)} %spread_ref.1, f32[12]{0:T(128)} %factor_ref.1, f32[128,128]{1,0:T(8,128)} %thermal_ref.1, ...), custom_call_target="tpu_custom_call" | custom-call | tf_op jit(solution)/shard_map/pallas_call | solution.py:470
  68.6 1.0 %copy.12 = f32[32,4,2048]{2,1,0:T(4,128)} copy(f32[32,4,2048]{2,1,0:T(4,128)S(1)} %get-tuple-element.4) | data formatting | bytes 2097152
  69.6 1.0 %copy.13 = f32[32,4,2048]{2,1,0:T(4,128)} copy(f32[32,4,2048]{2,1,0:T(4,128)S(1)} %get-tuple-element.5) | data formatting | bytes 2097152

commit v3 on v2

--- a/solution.py
+++ b/solution.py
@@ -16,6 +16,8 @@
 LANES = 128
 SLAB = 32
 PIECE = 272
+FIRST, LAST = 16, 16 + LANES
+SPAN = LAST + 16
 OFFSETS = [(h, l, c) for h in (0, 1) for l in (0, 1) for c in (0, 1)]
 
 
@@ -43,7 +45,7 @@
     pairs,
     heat_ref, wet_ref, label_ref, spread_ref, factor_ref, thermal_ref, water_ref, deriv_ref,
     heat_out, wet_out,
-    slab, block, piece, kloc, ksend, kgot, coef, kmid, state, solved, result, mats,
+    slab, block, piece, kloc, ksend, kgot, coef, turned, state, solved, result, mats,
     load_sem, own_sem, xsend, xrecv, zsend, zrecv, kown_sem, kx_sem, kz_sem, kzrecv, rown_sem, rsend, rrecv, store_sem,
 ):
     my_lat = lax.axis_index("lat")
@@ -140,9 +142,9 @@
                 packed = jnp.zeros((8, LANES), jnp.float32)
                 for r in range(4):
                     for q in range(4):
-                        g = r * 4 + q
+                        g = q * 4 + r
                         rows = pl.ds(q * 8, 8)
-                        block[t, pl.ds((f * 16 + g) * 8, 8), :] = slab[f, r, rows, pl.ds(here, LANES)]
+                        block[t, pl.ds((f * 16 + r * 4 + q) * 8, 8), :] = slab[f, r, rows, pl.ds(here, LANES)]
                         edge = jnp.where(
                             keep_right,
                             slab[f, r, rows, pl.ds(after, LANES)],
@@ -236,7 +238,7 @@
             device_id_type=MESH,
         )
 
-    near = [(0, 1, 0), (0, 1, 1), (1, 1, 0), (1, 1, 1)]
+    near = [(0, 1, 0), (1, 1, 0), (0, 1, 1), (1, 1, 1)]
     far = [(1, 0, 0), (1, 0, 1)]
     sibling = (0, 0, 1)
     remote = [sibling] + near + far
@@ -257,16 +259,12 @@
     for o in remote:
         x_copy(0, o).start()
     own_copy(0).start()
-    build(1)
     own_copy(0).wait()
     forward(0, (0, 0, 0), start)
+    build(1)
     own_copy(1).start()
-
-    highest = lax.Precision.HIGHEST
-    mats[0, :, 0:LEVELS] = thermal_ref[...]
-    mats[1, :, 0:LEVELS] = water_ref[...]
-    mats[0, :, LEVELS:] = -0.25 * jnp.dot(thermal_ref[...], deriv_ref[...], precision=highest, preferred_element_type=jnp.float32)
-    mats[1, :, LEVELS:] = 0.5 * jnp.dot(water_ref[...], deriv_ref[...], precision=highest, preferred_element_type=jnp.float32)
+    for o in remote:
+        x_copy(1, o).start()
 
     k_copy(1 - lo).wait_recv()
     k_forward(0, start)
@@ -294,59 +292,87 @@
                 device_id=(my_lat + 2, my_d), device_id_type=MESH,
             ).wait_recv()
 
-        for k in range(CHUNKS):
+    sub = lax.broadcasted_iota(jnp.int32, (8, LANES), 0)
+
+    def put_edges(edges, dst, row):
+        dst[row, FIRST - 8:FIRST] = jnp.where(sub >= 4, edges[(row + 15) % 16 * 8:(row + 15) % 16 * 8 + 8], 0.0)
+        dst[row, LAST:LAST + 8] = jnp.where(sub < 4, edges[row * 8:row * 8 + 8], 0.0)
+
+    def diffusivities(k):
+        for kind in range(2):
+            dst = coef.at[k, kind]
+
+            @pl.loop(0, 16)
+            def _(r):
+                line = kgot[r // 4, k, 0, pl.ds(kind * 4 + r % 4, 1), :]
+                dst[r, FIRST:LAST] = 0.25 * jnp.broadcast_to(line, (LANES, LANES)).T
+
+            edges = jnp.zeros((8, LANES), jnp.float32)
             for r in range(16):
-                for part in range(2):
-                    cols = slice(part * LANES, (part + 1) * LANES)
-                    kh = jnp.broadcast_to(kgot[r // 4, k, part, r % 4:r % 4 + 1, :], (8, LANES))
-                    km = jnp.broadcast_to(kgot[r // 4, k, part, 4 + r % 4:5 + r % 4, :], (8, LANES))
-                    coef[k, 0, r, :, cols] = 0.375 * kh
-                    coef[k, 1, r, :, cols] = 0.125 * kh
-                    coef[k, 2, r, :, cols] = 0.25 * km
-                    if part == 0 and 4 <= r < 12:
-                        half = slice(((r - 4) % 2) * LANES, ((r - 4) % 2 + 1) * LANES)
-                        kmid[k, (r - 4) // 2, :, half] = km
-
-    inside = jnp.logical_or(right, left)
-
-    def stencil(k, q):
-        d = flip(hi, q // 2) * 2 + flip(core, q % 2)
-
-        @pl.loop(0, 4)
-        def _(tile):
-            level = pl.multiple_of(d * SLAB + tile * 8, 8)
-
-            def load(r, f):
-                row = r % 4
-                main = piece[k, r // 4, q, pl.ds(pl.multiple_of((f * 16 + row * 4 + tile) * 8, 8), 8), :]
-                packed = piece[k, r // 4, q, pl.ds(256 + f * 8, 8), :]
-                shift = lax.rem(LANES - 8 * (row * 4 + tile), LANES)
-                edge = jnp.where(inside, pltpu.roll(packed, shift, 1), 0.0)
-                return jnp.concatenate([main, edge], axis=1)
-
-            def lap(rows, r):
-                centre = rows[r]
-                east = pltpu.roll(centre, 2 * LANES - 1, 1)
-                west = pltpu.roll(centre, 1, 1)
-                return rows[r + 1] + rows[r - 1] + east + west - 4.0 * centre
-
-            heat = [{} for _ in range(LSUB + 1)]
-            wet = [{} for _ in range(LSUB + 1)]
-            for front in range(16):
-                heat[0][front] = load(front, 0)
-                wet[0][front] = load(front, 1)
-                for t in range(1, LSUB + 1):
-                    r = front - t
-                    if r < t or r > 15 - t:
-                        continue
-                    h, w = heat[t - 1][r], wet[t - 1][r]
-                    factor = coef[k, 0, r] - coef[k, 1, r] / (1.0 + w * w)
-                    heat[t][r] = h + factor * lap(heat[t - 1], r)
-                    wet[t][r] = w + coef[k, 2, r] * lap(wet[t - 1], r)
-                    if t == LSUB:
-                        half = slice(((r - 4) % 2) * LANES, ((r - 4) % 2 + 1) * LANES)
-                        state[k, 0, (r - 4) // 2, pl.ds(level, 8), half] = heat[t][r][:, :LANES]
-                        state[k, 1, (r - 4) // 2, pl.ds(level, 8), half] = wet[t][r][:, :LANES]
+                line = jnp.broadcast_to(kgot[r // 4, k, 1, kind * 4 + r % 4:kind * 4 + r % 4 + 1, :], (8, LANES))
+                edges = edges + (pltpu.roll(line, 8 * r, 1) if r else line)
+            edges = 0.25 * jnp.broadcast_to(edges[0:1], (LANES, LANES)).T
+            for r in range(16):
+                put_edges(edges, dst, r)
+
+    def slot(d):
+        h2, c2 = d // 2, d % 2
+        return ((1 - hi) if h2 else hi) * 2 + ((1 - core) if c2 else core)
+
+    def turn(k, outer):
+        slots = [slot(d) for d in range(4)]
+
+        @pl.loop(0, 16)
+        def _(i):
+            f, r = i // 8, i % 8
+            row = (r + r // 4 * 8) if outer else r + 4
+            rows = pl.ds(pl.multiple_of(f * 128 + r % 4 * 32, 32), 32)
+            levels = jnp.concatenate([piece[k, row // 4, q, rows, :] for q in slots], axis=0)
+            turned[0, f, row, FIRST:LAST] = levels.T
+
+        if not outer:
+            return
+
+        for f in range(2):
+            blocks = []
+            for q in slots:
+                packs = [piece[k, strip, q, 256 + f * 8:264 + f * 8, :] for strip in range(4)]
+                for tile in range(4):
+                    total = jnp.zeros((8, LANES), jnp.float32)
+                    for strip in range(4):
+                        shift = 32 * (strip - tile) % LANES
+                        moved = pltpu.roll(packs[strip], shift, 1) if shift else packs[strip]
+                        inside = (lane + 4) % LANES // 32 == strip
+                        total = jnp.where(inside, moved, total)
+                    blocks.append(total)
+            edges = jnp.concatenate(blocks, axis=0).T
+            for r in range(16):
+                put_edges(edges, turned.at[0, f], r)
+
+    def stencil(k):
+        for t in range(LSUB):
+            src, dst = turned.at[t % 2], turned.at[1 - t % 2]
+            last = t == LSUB - 1
+
+            @pl.loop(t + 1, 15 - t)
+            def _(r):
+                for s in range(FIRST if last else FIRST - 8, LAST if last else LAST + 8, 8):
+                    def lap(f, centre):
+                        return (
+                            src[f, r + 1, s:s + 8] + src[f, r - 1, s:s + 8]
+                            + src[f, r, s + 1:s + 9] + src[f, r, s - 1:s + 7] - 4.0 * centre
+                        )
+
+                    h, w = src[0, r, s:s + 8], src[1, r, s:s + 8]
+                    factor = coef[k, 0, r, s:s + 8] * (1.5 - 0.5 / (1.0 + w * w))
+                    h2 = h + factor * lap(0, h)
+                    w2 = w + coef[k, 1, r, s:s + 8] * lap(1, w)
+                    if last:
+                        state[k, 0, r - 4, s - FIRST:s - FIRST + 8] = h2
+                        state[k, 1, r - 4, s - FIRST:s - FIRST + 8] = w2
+                    else:
+                        dst[0, r, s:s + 8] = h2
+                        dst[1, r, s:s + 8] = w2
 
     def r_copy(k, half, o):
         lo2, d2, dev = place(o)
@@ -384,11 +410,19 @@
         for half in range(2):
             for l in (1, 0):
                 rp = flip(lo, l) * 2 + half
-                h = state[k, 0, rp]
-                w = state[k, 1, rp]
-                kw = w * kmid[k, rp, 0:1, :]
-                temp = jnp.dot(mats[0], jnp.concatenate([h, kw], axis=0), precision=highest, preferred_element_type=jnp.float32)
-                moist = jnp.dot(mats[1], jnp.concatenate([w, kw], axis=0), precision=highest, preferred_element_type=jnp.float32)
+                fields = [[], []]
+                for r in range(2):
+                    h, w = state[k, 0, rp * 2 + r], state[k, 1, rp * 2 + r]
+                    kw = w * coef[k, 1, rp * 2 + r + 4, FIRST:LAST]
+                    fields[0].append(jnp.concatenate([h, kw], axis=1))
+                    fields[1].append(jnp.concatenate([w, kw], axis=1))
+                temp, moist = (
+                    lax.dot_general(
+                        mats[n], jnp.concatenate(fields[n], axis=0), (((1,), (1,)), ((), ())),
+                        precision=highest, preferred_element_type=jnp.float32,
+                    )
+                    for n in range(2)
+                )
                 for f, out in enumerate((temp, moist)):
                     solved[k, f, rp * 2] = out[:, :LANES]
                     solved[k, f, rp * 2 + 1] = out[:, LANES:]
@@ -398,31 +432,40 @@
                     else:
                         r_copy(k, half, o).start()
 
-    for o in near:
-        arrive(0, o)
-    for o in remote:
-        x_copy(1, o).start()
-    forward(1, (0, 0, 0), start)
+    k_received()
+    arrive(0, near[0])
+    arrive(0, near[1])
+    diffusivities(0)
+    arrive(0, near[2])
+    arrive(0, near[3])
+    diffusivities(1)
+    highest = lax.Precision.HIGHEST
+    mats[0, :, 0:LEVELS] = thermal_ref[...]
+    mats[1, :, 0:LEVELS] = water_ref[...]
+    mats[0, :, LEVELS:] = -1.0 * jnp.dot(thermal_ref[...], deriv_ref[...], precision=highest, preferred_element_type=jnp.float32)
+    mats[1, :, LEVELS:] = 2.0 * jnp.dot(water_ref[...], deriv_ref[...], precision=highest, preferred_element_type=jnp.float32)
+
     for o in far:
         arrive(0, o)
-    k_received()
+    forward(1, (0, 0, 0), start)
     arrive(1, sibling)
-    halo_wait(0, 0)
-    stencil(0, 0)
-    halo_wait(0, 1)
-    stencil(0, 1)
-    halo_wait(0, 2)
-    stencil(0, 2)
-    for o in near:
-        arrive(1, o)
-    halo_wait(0, 3)
-    stencil(0, 3)
+    turn(0, False)
+    arrive(1, near[0])
+    arrive(1, near[1])
+    for q in range(4):
+        halo_wait(0, q)
+    turn(0, True)
+    stencil(0)
+    arrive(1, near[2])
+    arrive(1, near[3])
     solve(0)
     for o in far:
         arrive(1, o)
+    turn(1, False)
     for q in range(4):
         halo_wait(1, q)
-        stencil(1, q)
+    turn(1, True)
+    stencil(1)
     solve(1)
 
     def store(k):
@@ -479,9 +522,9 @@
                 pltpu.VMEM((18, 8, LANES), f32),
                 pltpu.VMEM((CHUNKS, 2, 8, LANES), f32),
                 pltpu.VMEM((4, CHUNKS, 2, 8, LANES), f32),
-                pltpu.VMEM((CHUNKS, 3, 16, 8, 2 * LANES), f32),
-                pltpu.VMEM((CHUNKS, 4, 8, 2 * LANES), f32),
-                pltpu.VMEM((CHUNKS, 2, 4, LEVELS, 2 * LANES), f32),
+                pltpu.VMEM((CHUNKS, 2, 16, SPAN, LANES), f32),
+                pltpu.VMEM((2, 2, 16, SPAN, LANES), f32),
+                pltpu.VMEM((CHUNKS, 2, 8, LANES, LEVELS), f32),
                 pltpu.VMEM((CHUNKS, 2, 8, LEVELS, LANES), f32),
                 pltpu.VMEM((2, 4, SLAB, 16 * LANES), f32),
                 pltpu.VMEM((2, LEVELS, 2 * LEVELS), f32),

time: 70.7 us -> 67.6 us (0.956); the launches traced: 70.6 us -> 66.7 us
  Pallas kernels: 68 us -> 64.1 us
    pallas_call x1, Pallas kernels: 68 us -> 64.1 us  [per_device(): pl.pallas_call(functools.partial(kernel, pairs), out_shape=(out, out), in...]
where the time goes in v3:
time: 67.6 us; the launch traced here: 66.7 us
  Pallas kernels  64.1 us (95%)
  local copies, waits for them, and re-layouts  1.94 us (3%)
    pallas_call x1, Pallas kernels, per_device(): pl.pallas_call(functools.partial(kernel, pairs), out_shape=(out, out), in...  64.1 us
    unnamed x2, local copies, waits for them, and re-layouts  1.94 us

profile of v3, /device:TPU:25, one launch (start us, length us, event | category | flops | bytes accessed | tf_op | source)
XLA Modules:
  0.0 66.7 jit_solution(4118227595156650314)
XLA Ops:
  0.6 64.1 %shard_map.95 = (f32[32,4,2048]{2,1,0:T(4,128)S(1)}, f32[32,4,2048]{2,1,0:T(4,128)S(1)}) custom-call(f32[32,4,2048]{2,1,0:T(4,128)} %heat_ref.1, f32[32,4,2048]{2,1,0:T(4,128)} %wet_ref.1, s32[4,2048]{1,0:T(4,128)} %label_ref.1, f32[12]{0:T(128)} %spread_ref.1, f32[12]{0:T(128)} %factor_ref.1, f32[128,128]{1,0:T(8,128)} %thermal_ref.1, ...), custom_call_target="tpu_custom_call" | custom-call | tf_op jit(solution)/shard_map/pallas_call | solution.py:513
  64.8 1.0 %copy.12 = f32[32,4,2048]{2,1,0:T(4,128)} copy(f32[32,4,2048]{2,1,0:T(4,128)S(1)} %get-tuple-element.4) | data formatting | bytes 2097152
  65.8 1.0 %copy.13 = f32[32,4,2048]{2,1,0:T(4,128)} copy(f32[32,4,2048]{2,1,0:T(4,128)S(1)} %get-tuple-element.5) | data formatting | bytes 2097152

commit v4 on v3

--- a/solution.py
+++ b/solution.py
@@ -203,16 +203,24 @@
         def _():
             act(forward_copy(k, o, 1))
 
-    def halo_wait(k, q):
-        o = (q // 2, 0, q % 2)
-
-        @pl.when(has_after)
-        def _():
-            forward_copy(k, o, 0).wait_recv()
-
-        @pl.when(has_before)
-        def _():
-            forward_copy(k, o, 1).wait_recv()
+    def halo_wait(k, late):
+        for q in range(4):
+            o = (q // 2, 0, q % 2)
+
+            @pl.when(jnp.logical_and(has_after, lo == (0 if late else 1)))
+            def _():
+                forward_copy(k, o, 0).wait_recv()
+
+            @pl.when(jnp.logical_and(has_before, lo == (1 if late else 0)))
+            def _():
+                forward_copy(k, o, 1).wait_recv()
+
+    def turn_halos(k):
+        halo_wait(k, False)
+        turn(k, lo * 12, 4)
+        halo_wait(k, True)
+        turn(k, (1 - lo) * 12, 4)
+        turn_edges(k)
 
     def k_forward(s, act):
         @pl.when(has_before if s == 0 else has_after)
@@ -319,20 +327,18 @@
         h2, c2 = d // 2, d % 2
         return ((1 - hi) if h2 else hi) * 2 + ((1 - core) if c2 else core)
 
-    def turn(k, outer):
+    def turn(k, first, count):
         slots = [slot(d) for d in range(4)]
 
-        @pl.loop(0, 16)
+        @pl.loop(0, 2 * count)
         def _(i):
-            f, r = i // 8, i % 8
-            row = (r + r // 4 * 8) if outer else r + 4
-            rows = pl.ds(pl.multiple_of(f * 128 + r % 4 * 32, 32), 32)
+            f, row = i // count, first + i % count
+            rows = pl.ds(pl.multiple_of(f * 128 + row % 4 * 32, 32), 32)
             levels = jnp.concatenate([piece[k, row // 4, q, rows, :] for q in slots], axis=0)
             turned[0, f, row, FIRST:LAST] = levels.T
 
-        if not outer:
-            return
-
+    def turn_edges(k):
+        slots = [slot(d) for d in range(4)]
         for f in range(2):
             blocks = []
             for q in slots:
@@ -449,30 +455,26 @@
         arrive(0, o)
     forward(1, (0, 0, 0), start)
     arrive(1, sibling)
-    turn(0, False)
+    turn(0, 4, 8)
     arrive(1, near[0])
     arrive(1, near[1])
-    for q in range(4):
-        halo_wait(0, q)
-    turn(0, True)
-    stencil(0)
+    turn_halos(0)
     arrive(1, near[2])
     arrive(1, near[3])
+    stencil(0)
+    arrive(1, far[0])
     solve(0)
-    for o in far:
-        arrive(1, o)
-    turn(1, False)
-    for q in range(4):
-        halo_wait(1, q)
-    turn(1, True)
+    arrive(1, far[1])
+    turn(1, 4, 8)
+    turn_halos(1)
     stencil(1)
     solve(1)
 
-    def store(k):
+    def store(k, half):
         cols = pl.ds(k * 8 * LANES, 8 * LANES)
         copies = []
         for f, out in enumerate((heat_out, wet_out)):
-            for r in range(4):
+            for r in (half * 2, half * 2 + 1):
                 copies.append(pltpu.make_async_copy(result.at[f, r, :, cols], out.at[:, r, cols], store_sem.at[k, f * 4 + r]))
         return copies
 
@@ -481,8 +483,8 @@
             r_own(k, half).wait()
             for o in remote:
                 r_arrival(k, half, o).wait_recv()
-        for cp in store(k):
-            cp.start()
+            for cp in store(k, half):
+                cp.start()
 
     k_copy(lo).wait_send()
     k_forward(0, lambda cp: cp.wait_send())
@@ -495,8 +497,8 @@
         for half in range(2):
             for o in remote:
                 r_copy(k, half, o).wait_send()
-        for cp in store(k):
-            cp.wait()
+            for cp in store(k, half):
+                cp.wait()
 
 
 def solution(mesh):

time: 67.6 us -> 64.7 us (0.957)
  the two profiles are of different devices: /device:TPU:25 before, /device:TPU:65 now
where the time goes in v4:
time: 64.7 us; the launch traced here: 64.6 us
  Pallas kernels  62 us (96%)
  local copies, waits for them, and re-layouts  1.94 us (3%)
    pallas_call x1, Pallas kernels, per_device(): pl.pallas_call(functools.partial(kernel, pairs), out_shape=(out, out), in...  62 us
    unnamed x2, local copies, waits for them, and re-layouts  1.94 us

profile of v4, /device:TPU:65, one launch (start us, length us, event | category | flops | bytes accessed | tf_op | source)
XLA Modules:
  0.0 64.6 jit_solution(420129901233381503)
XLA Ops:
  0.6 62.0 %shard_map.95 = (f32[32,4,2048]{2,1,0:T(4,128)S(1)}, f32[32,4,2048]{2,1,0:T(4,128)S(1)}) custom-call(f32[32,4,2048]{2,1,0:T(4,128)} %heat_ref.1, f32[32,4,2048]{2,1,0:T(4,128)} %wet_ref.1, s32[4,2048]{1,0:T(4,128)} %label_ref.1, f32[12]{0:T(128)} %spread_ref.1, f32[12]{0:T(128)} %factor_ref.1, f32[128,128]{1,0:T(8,128)} %thermal_ref.1, ...), custom_call_target="tpu_custom_call" | custom-call | tf_op jit(solution)/shard_map/pallas_call | solution.py:515
  62.6 1.0 %copy.12 = f32[32,4,2048]{2,1,0:T(4,128)} copy(f32[32,4,2048]{2,1,0:T(4,128)S(1)} %get-tuple-element.4) | data formatting | bytes 2097152
  63.6 1.0 %copy.13 = f32[32,4,2048]{2,1,0:T(4,128)} copy(f32[32,4,2048]{2,1,0:T(4,128)S(1)} %get-tuple-element.5) | data formatting | bytes 2097152

commit v5 on v4

--- a/solution.py
+++ b/solution.py
@@ -414,7 +414,7 @@
 
     def solve(k):
         for half in range(2):
-            for l in (1, 0):
+            for l in (0, 1):
                 rp = flip(lo, l) * 2 + half
                 fields = [[], []]
                 for r in range(2):

time: 64.7 us -> 64.5 us (level)
  the two profiles are of different devices: /device:TPU:65 before, /device:TPU:25 now
where the time goes in v5:
time: 64.5 us; the launch traced here: 64 us
  Pallas kernels  61.4 us (95%)
  local copies, waits for them, and re-layouts  1.94 us (3%)
    pallas_call x1, Pallas kernels, per_device(): pl.pallas_call(functools.partial(kernel, pairs), out_shape=(out, out), in...  61.4 us
    unnamed x2, local copies, waits for them, and re-layouts  1.94 us

profile of v5, /device:TPU:25, one launch (start us, length us, event | category | flops | bytes accessed | tf_op | source)
XLA Modules:
  0.0 64.0 jit_solution(3531311668063059746)
XLA Ops:
  0.6 61.4 %shard_map.95 = (f32[32,4,2048]{2,1,0:T(4,128)S(1)}, f32[32,4,2048]{2,1,0:T(4,128)S(1)}) custom-call(f32[32,4,2048]{2,1,0:T(4,128)} %heat_ref.1, f32[32,4,2048]{2,1,0:T(4,128)} %wet_ref.1, s32[4,2048]{1,0:T(4,128)} %label_ref.1, f32[12]{0:T(128)} %spread_ref.1, f32[12]{0:T(128)} %factor_ref.1, f32[128,128]{1,0:T(8,128)} %thermal_ref.1, ...), custom_call_target="tpu_custom_call" | custom-call | tf_op jit(solution)/shard_map/pallas_call | solution.py:515
  62.0 1.0 %copy.12 = f32[32,4,2048]{2,1,0:T(4,128)} copy(f32[32,4,2048]{2,1,0:T(4,128)S(1)} %get-tuple-element.4) | data formatting | bytes 2097152
  63.0 1.0 %copy.13 = f32[32,4,2048]{2,1,0:T(4,128)} copy(f32[32,4,2048]{2,1,0:T(4,128)S(1)} %get-tuple-element.5) | data formatting | bytes 2097152
